TPU v7x, 32 devices: a whole 2x2x4 slice. The times are simulated.
32 devices in a mesh: groups: 2 (over y), fsdp: 2 (over core), ep: 8 (over z, x).
Axes of the slice: x: 2, y: 2, z: 4, core: 2. Of those that a mesh axis runs over, the one named last changes fastest.
Arguments:
- tokens: bfloat16 [32, 7168], P(('groups', 'fsdp', 'ep')), parts along dimension 0, may hold values from -6 to 6
- gate_weight: bfloat16 [7168, 1024], P('fsdp', 'ep'), may hold values from -0.0625 to 0.0625
- up_weight: bfloat16 [7168, 1024], P('fsdp', 'ep'), may hold values from -0.0625 to 0.0625
- down_weight: bfloat16 [1024, 7168], P('ep', 'fsdp'), may hold values from -0.1875 to 0.1875
- steering: bfloat16 [1, 7168], replicated, may hold values from -3 to 3
- block_rows: int32 [2, 2, 8], P(None, 'groups'), parts along dimension 1, may hold values from 0 to 7, as said below
- block_gates: float32 [2, 2, 8], P(None, 'groups'), parts along dimension 1, may hold values from 0 to 1, as said below
Outputs:
- mixed: bfloat16 [32, 7168], P(('groups', 'fsdp', 'ep')), parts along dimension 0
There are 2 independent parts, one for each index of `groups`. A program takes and returns all parts, laid end to end along the dimension named above; an argument that names none is the same for every part. Nothing has to cross between parts.
Inputs may be any that keep to these rules, and one draw needn't show every extreme that they name: `block_rows`: within one block the 8 token numbers are distinct. `block_gates`: in each block the gates are positive and falling on the first slots and zero on the rest; in each half one block has no zero gate.
All inputs are finite; a program needn't handle non-finite values.
Results may differ from a plain program's by a relative error of at most 0.0049.
Values may be sent and summed in bfloat16 or wider, within the bound.
No kernel may reach another device: no remote copies, remote signals or barrier semaphores. Data moves between devices by JAX's collectives and lax.ppermute only.
A program may use at most 64 MiB of HBM per device.

v0:
```python
import jax
import jax.numpy as jnp
from jax import lax
from jax.sharding import PartitionSpec as P


def body(tokens, gate_weight, up_weight, down_weight, steering, block_rows, block_gates):
    tok_rows = lax.all_gather(tokens, "ep", axis=0, tiled=True)
    slice_units = gate_weight.shape[1]
    window_experts = block_rows.shape[1]
    ep_count = lax.axis_size("ep")
    window_width = ep_count * slice_units // window_experts
    group_size = window_width // slice_units
    position = lax.axis_index("ep")
    expert = position // group_size
    member = position % group_size
    half_index = lax.axis_index("fsdp")
    expert_rows = lax.dynamic_index_in_dim(block_rows, expert, 1, keepdims=False)
    expert_gates = lax.dynamic_index_in_dim(block_gates, expert, 1, keepdims=False)
    slot_rows = lax.dynamic_index_in_dim(expert_rows, half_index, 0, keepdims=False)
    slot_gates = lax.dynamic_index_in_dim(expert_gates, half_index, 0, keepdims=False)
    picked = jnp.take(tok_rows, slot_rows, axis=0)
    gate_pre = jnp.dot(
        picked,
        lax.all_gather(gate_weight, "fsdp", axis=0, tiled=True),
        preferred_element_type=jnp.float32,
    )
    up_pre = jnp.dot(
        picked,
        lax.all_gather(up_weight, "fsdp", axis=0, tiled=True),
        preferred_element_type=jnp.float32,
    )
    hidden = (jax.nn.silu(gate_pre) * up_pre).astype(jnp.bfloat16)
    half_rows = tok_rows.shape[0]
    width_all = tok_rows.shape[1]
    steer_row = lax.dynamic_index_in_dim(steering, expert, 0, keepdims=False).astype(jnp.float32)
    projected = jnp.dot(
        hidden,
        lax.all_gather(down_weight, "fsdp", axis=1, tiled=True),
        preferred_element_type=jnp.float32,
    )
    leader = (member == 0).astype(jnp.float32)
    weighted = slot_gates[:, None] * (projected + leader * steer_row[None, :])
    partial_sum = jnp.zeros((half_rows, width_all), jnp.float32).at[slot_rows].add(weighted)
    summed = lax.psum_scatter(partial_sum, "ep", scatter_dimension=0, tiled=True)
    return summed.astype(jnp.bfloat16)


def solution(mesh):
    placed = (
        P(("groups", "fsdp", "ep"), None),
        P("fsdp", "ep"),
        P("fsdp", "ep"),
        P("ep", "fsdp"),
        P(),
        P(None, "groups", None),
        P(None, "groups", None),
    )
    return jax.shard_map(
        body,
        mesh=mesh,
        in_specs=placed,
        out_specs=P(("groups", "fsdp", "ep"), None),
        check_vma=False,
    )
```

profile of v0, /device:TPU:0, one launch (start us, length us, event | category | flops | bytes accessed | tf_op | source)
XLA Modules:
  0.0 99.3 jit_solution(15042454936637568538)
XLA Ops:
  6.5 0.0 copy-start
  6.5 0.0 copy-start.3
  6.5 0.0 copy-start.2
  6.5 0.0 all-gather.5.cloned.1.call-start
  6.5 0.7 all-gather.5.cloned.1.call-update
  7.3 0.0 copy-start.4
  7.3 0.0 copy-start.1
  7.3 0.0 all-gather.7.cloned.1.call-start
  7.3 0.7 all-gather.7.cloned.1.call-update
  8.0 0.0 all-gather.9.cloned.1.call-start
  8.1 0.7 all-gather.9.cloned.1.call-update
  8.8 0.0 copy-done.3
  8.9 0.0 copy-done.2
  8.9 32.5 %all-gather = bf16[8,1,7168]{2,1,0:T(2,128)(2,1)S(1)} all-gather(bf16[1,1,7168]{2,1,0:T(2,128)(2,1)S(1)} %bitcast.19), channel_id=1, replica_groups=mesh['groups'=2,'fsdp'=2,'ep'=8] {'ep'}, dimensions={0}, use_global_device_ids=true | all-gather | bytes 129024 | tf_op jit(solution)/shard_map/all_gather | solution.py:8
  41.4 0.0 copy-done
  41.4 0.6 gather_fusion
  42.0 0.0 copy-done.4
  42.1 0.6 dynamic-slice.2
  42.6 0.0 copy-done.1
  42.7 0.0 all-gather.5.cloned.1.call-done
  42.7 2.0 %fusion.4 = f32[8,128]{1,0:T(8,128)S(1)} fusion(bf16[7168,128]{1,0:T(8,128)(2,1)} %all-gather.5.cloned.1.call-done, bf16[8,7168]{1,0:T(8,128)(2,1)S(1)} %gather_fusion, pred[8]{0:T(512)(128)(4,1)S(1)} %compare_and_fusion), kind=kOutput, calls=%fused_computation.10 | convolution fusion | flops 14737408 | bytes 1953800 | tf_op jit(solution)/shard_map/dot_general | solution.py:23
  44.7 0.0 all-gather.7.cloned.1.call-done
  44.8 2.9 %all-gather.9.cloned.1.call-done = bf16[128,7168]{1,0:T(8,128)(2,1)} async-done(((bf16[128,3584]{1,0:T(8,128)(2,1)}), bf16[128,7168]{1,0:T(8,128)(2,1)}) %all-gather.9.cloned.1.call-update) | async-done | bytes 1835024 | tf_op jit(solution)/shard_map/all_gather | solution.py:39
  47.7 2.8 %fusion = f32[8,7168]{1,0:T(8,128)S(1)} fusion(bf16[128,7168]{1,0:T(8,128)(2,1)} %all-gather.9.cloned.1.call-done, bf16[7168,128]{1,0:T(8,128)(2,1)} %all-gather.7.cloned.1.call-done, f32[7168]{0:T(1024)S(1)} %bitcast.18, f32[8]{0:T(128)S(1)} %dynamic-slice_bitcast_fusion, bf16[8,7168]{1,0:T(8,128)(2,1)S(1)} %gather_fusion, ...), kind=kOutput, calls=%fused_computation.3 | convolution fusion | flops 29538304 | bytes 4046888 | tf_op jit(solution)/shard_map/dot_general | solution.py:37
  50.5 0.9 scatter_custom_fusion
  51.4 40.1 %all-reduce.2 = bf16[8,7168]{1,0:T(8,128)(2,1)S(1)} all-reduce(f32[8,7168]{1,0:T(8,128)S(1)} %scatter_custom_fusion), channel_id=2, replica_groups=mesh['groups'=2,'fsdp'=2,'ep'=8] {'ep'}, use_global_device_ids=true, to_apply=%region_1.2.clone | all-reduce | flops 57344 | bytes 344064
  91.5 1.2 %dynamic-slice_convert_fusion = bf16[1,7168]{1,0:T(2,128)(2,1)} fusion(bf16[8,7168]{1,0:T(8,128)(2,1)S(1)} %all-reduce.2, u32[]{:T(128)} %bitcast.6), kind=kLoop, calls=%fused_computation.11 | loop fusion | bytes 28676 | tf_op jit(solution)/shard_map/convert_element_type | solution.py:46
  (6 shorter events, 0.1 us)
Async XLA Ops:
  6.5 34.9 %copy-start = (f32[2,1,8]{2,1,0:T(1,128)S(1)}, f32[2,1,8]{2,1,0:T(1,128)}, u32[]{:S(2)}) copy-start(f32[2,1,8]{2,1,0:T(1,128)} %param.13) | copy-start | bytes 196
  6.5 2.2 %copy-start.3 = (s32[2,1,8]{2,1,0:T(1,128)S(1)}, s32[2,1,8]{2,1,0:T(1,128)}, u32[]{:S(2)}) copy-start(s32[2,1,8]{2,1,0:T(1,128)} %param.12) | copy-start | bytes 196
  6.5 2.3 %copy-start.2 = (bf16[1,7168]{1,0:T(2,128)(2,1)S(1)}, bf16[1,7168]{1,0:T(2,128)(2,1)}, u32[]{:S(2)}) copy-start(bf16[1,7168]{1,0:T(2,128)(2,1)} %param.7) | copy-start | bytes 43012
  6.5 36.1 %all-gather.5.cloned.1.call-start = ((), (), s32[]{:S(2)}) async-start(), calls=%async_computation | async-start | bytes 2752512 | tf_op jit(solution)/shard_map/all_gather | solution.py:25
  7.3 34.8 %copy-start.4 = (u32[32]{0:T(128)S(1)}, u32[32]{0:T(128)}, u32[]{:S(2)}) copy-start(u32[32]{0:T(128)} %constant.79) | copy-start | bytes 388
  7.3 35.4 %copy-start.1 = (bf16[1,7168]{1,0:T(2,128)(2,1)S(1)}, bf16[1,7168]{1,0:T(2,128)(2,1)}, u32[]{:S(2)}) copy-start(bf16[1,7168]{1,0:T(2,128)(2,1)} %param.11) | copy-start | bytes 43012
  7.3 37.5 %all-gather.7.cloned.1.call-start = ((), (), s32[]{:S(2)}) async-start(), calls=%async_computation.1 | async-start | bytes 2752512 | tf_op jit(solution)/shard_map/all_gather | solution.py:30
  8.0 39.7 %all-gather.9.cloned.1.call-start = ((), (), s32[]{:S(2)}) async-start(), calls=%async_computation.2 | async-start | bytes 2752512 | tf_op jit(solution)/shard_map/all_gather | solution.py:39
Sparse Core Ops, SparseCore 0:
  8.9 12.8 all-gather.4
  23.4 11.3 all-gather.6
  36.3 11.3 all-gather.8
where the time goes:
time: 99.5 us; the launch traced here: 99.3 us
  blocking collectives  72.6 us (73%)
  between operations  13.3 us (13%)
  waiting for transfers between devices  5.06 us (5%)
  matrix products  4.84 us (5%)
  local copies, waits for them, and re-layouts  2.47 us (2%)
    unnamed x1, blocking collectives  40.1 us
    all_gather x1, blocking collectives, body(): tok_rows = lax.all_gather(tokens, 'ep', axis=0, tiled=True)  32.5 us
    all_gather x1, waiting for transfers between devices, body(): lax.all_gather(down_weight, 'fsdp', axis=1, tiled=True)  2.95 us
    dot_general x1, matrix products, body(): jnp.dot(hidden, lax.all_gather(down_weight, 'fsdp', axis=1, tiled=True),...  2.79 us
    unnamed x3, waiting for transfers between devices  2.08 us
    dot_general x1, matrix products, body(): jnp.dot(picked, lax.all_gather(gate_weight, 'fsdp', axis=0, tiled=True),...  2.05 us
  transfers between devices with their start and end apart: 3, of which 1 were waited for; matrix products, arithmetic and copies ran while one was open for 3% of the time, Pallas kernels for 0%

commit v1 on v0

--- a/solution.py
+++ b/solution.py
@@ -5,7 +5,17 @@
 
 
 def body(tokens, gate_weight, up_weight, down_weight, steering, block_rows, block_gates):
-    tok_rows = lax.all_gather(tokens, "ep", axis=0, tiled=True)
+    lanes = [tokens]
+    pp = 0
+    dev_count = jax.lax.psum(1, "ep")
+    while pp < dev_count - 1:
+        piece_now = jax.lax.ppermute(
+            lanes[-1], "ep", [(ix, (ix + 1) % dev_count) for ix in range(dev_count)]
+        )
+        lanes.append(piece_now)
+        pp += 1
+    right_arr = jnp.concatenate(lanes[::-1], axis=0)
+    tok_rows = jnp.roll(right_arr, shift=(jax.lax.axis_index("ep") + 1) * tokens.shape[0], axis=0)
     slice_units = gate_weight.shape[1]
     window_experts = block_rows.shape[1]
     ep_count = lax.axis_size("ep")

time: 99.5 us -> 106 us (1.065)
  waiting for transfers between devices: 5.06 us -> 45.2 us
  blocking collectives: 72.6 us -> 35.3 us
  starting transfers between devices: 0.08 us -> 3.12 us
    ppermute x0 -> x7, waiting for transfers between devices: none -> 43.7 us  [body(): jax.lax.ppermute(lanes[-1], 'ep', [(ix, (ix + 1) % dev_count) for ix in r...]
    all_gather x1 -> x0, blocking collectives: 32.5 us -> none  [body(): tok_rows = lax.all_gather(tokens, 'ep', axis=0, tiled=True)]
    unnamed x1, blocking collectives: 40.1 us -> 35.3 us
    ppermute x0 -> x7, starting transfers between devices: none -> 3.01 us  [body(): jax.lax.ppermute(lanes[-1], 'ep', [(ix, (ix + 1) % dev_count) for ix in r...]
    all_gather x1, waiting for transfers between devices: 2.95 us -> 0.02 us  [body(): lax.all_gather(down_weight, 'fsdp', axis=1, tiled=True)]
  transfers between devices with their start and end apart: 3 -> 10, of which waited for: 1 -> 7; matrix products, arithmetic and copies ran while one was open for 3% -> 4% of each run, Pallas kernels for 0% -> 0%
where the time goes in v1:
time: 106 us
  waiting for transfers between devices  45.2 us (43%)
  blocking collectives  35.3 us (33%)
  between operations  13.3 us (13%)
  matrix products  4.69 us (4%)
  local copies, waits for them, and re-layouts  3.34 us (3%)
  starting transfers between devices  3.12 us (3%)
    ppermute x7, waiting for transfers between devices, body(): jax.lax.ppermute(lanes[-1], 'ep', [(ix, (ix + 1) % dev_count) for ix in r...  43.7 us
    unnamed x1, blocking collectives  35.3 us
    ppermute x7, starting transfers between devices, body(): jax.lax.ppermute(lanes[-1], 'ep', [(ix, (ix + 1) % dev_count) for ix in r...  3.01 us
    dot_general x1, matrix products, body(): jnp.dot(hidden, lax.all_gather(down_weight, 'fsdp', axis=1, tiled=True),...  2.79 us
  transfers between devices with their start and end apart: 10, of which 7 were waited for; matrix products, arithmetic and copies ran while one was open for 4% of the time, Pallas kernels for 0%

profile of v1, /device:TPU:0, one launch (start us, length us, event | category | flops | bytes accessed | tf_op | source)
XLA Modules:
  0.0 105.9 jit_solution(6184102733772753001)
XLA Ops:
  6.5 0.0 copy-start
  6.5 0.0 copy-start.4
  6.5 0.0 copy-start.1
  6.5 0.0 copy-start.2
  6.5 0.0 copy-start.3
  6.5 0.0 all-gather.4.cloned.1.call-start
  6.6 0.7 all-gather.4.cloned.1.call-update
  7.3 0.0 all-gather.6.cloned.1.call-start
  7.3 0.7 all-gather.6.cloned.1.call-update
  8.0 0.0 all-gather.8.cloned.1.call-start
  8.1 0.0 copy-done.1
  8.1 3.0 %collective-permute-start = (bf16[1,7168]{1,0:T(2,128)(2,1)S(1)}, bf16[1,7168]{1,0:T(2,128)(2,1)S(1)}, u32[]{:S(2)}, u32[]{:S(2)}) collective-permute-start(bf16[1,7168]{1,0:T(2,128)(2,1)S(1)} %copy-done.1), channel_id=1, source_target_pairs={{0,1},{1,2},{2,3},{3,4},{4,5},{5,6},{6,7},{7,0},{8,9},{9,10},{10,1... | collective-permute-start | bytes 43016 | tf_op jit(solution)/shard_map/ppermute | solution.py:12
  11.1 4.9 %collective-permute-done = bf16[1,7168]{1,0:T(2,128)(2,1)S(1)} collective-permute-done((bf16[1,7168]{1,0:T(2,128)(2,1)S(1)}, bf16[1,7168]{1,0:T(2,128)(2,1)S(1)}, u32[]{:S(2)}, u32[]{:S(2)}) %collective-permute-start) | collective-permute-done | bytes 14368 | tf_op jit(solution)/shard_map/ppermute | solution.py:12
  16.0 0.0 collective-permute-start.1
  16.0 0.0 all-gather.8.cloned.1.call-update
  16.0 6.5 %collective-permute-done.1 = bf16[1,7168]{1,0:T(2,128)(2,1)S(1)} collective-permute-done((bf16[1,7168]{1,0:T(2,128)(2,1)S(1)}, bf16[1,7168]{1,0:T(2,128)(2,1)S(1)}, u32[]{:S(2)}, u32[]{:S(2)}) %collective-permute-start.1) | collective-permute-done | bytes 14368 | tf_op jit(solution)/shard_map/ppermute | solution.py:12
  22.5 0.0 collective-permute-start.2
  22.5 0.0 copy-done.2
  22.6 6.5 %collective-permute-done.2 = bf16[1,7168]{1,0:T(2,128)(2,1)S(1)} collective-permute-done((bf16[1,7168]{1,0:T(2,128)(2,1)S(1)}, bf16[1,7168]{1,0:T(2,128)(2,1)S(1)}, u32[]{:S(2)}, u32[]{:S(2)}) %collective-permute-start.2) | collective-permute-done | bytes 14368 | tf_op jit(solution)/shard_map/ppermute | solution.py:12
  29.1 0.0 collective-permute-start.3
  29.1 0.0 copy-done.3
  29.1 6.6 %collective-permute-done.3 = bf16[1,7168]{1,0:T(2,128)(2,1)S(1)} collective-permute-done((bf16[1,7168]{1,0:T(2,128)(2,1)S(1)}, bf16[1,7168]{1,0:T(2,128)(2,1)S(1)}, u32[]{:S(2)}, u32[]{:S(2)}) %collective-permute-start.3) | collective-permute-done | bytes 14368 | tf_op jit(solution)/shard_map/ppermute | solution.py:12
  35.7 0.0 collective-permute-start.4
  35.7 6.8 %collective-permute-done.4 = bf16[1,7168]{1,0:T(2,128)(2,1)S(1)} collective-permute-done((bf16[1,7168]{1,0:T(2,128)(2,1)S(1)}, bf16[1,7168]{1,0:T(2,128)(2,1)S(1)}, u32[]{:S(2)}, u32[]{:S(2)}) %collective-permute-start.4) | collective-permute-done | bytes 14368 | tf_op jit(solution)/shard_map/ppermute | solution.py:12
  42.5 0.0 collective-permute-start.5
  42.5 6.6 %collective-permute-done.5 = bf16[1,7168]{1,0:T(2,128)(2,1)S(1)} collective-permute-done((bf16[1,7168]{1,0:T(2,128)(2,1)S(1)}, bf16[1,7168]{1,0:T(2,128)(2,1)S(1)}, u32[]{:S(2)}, u32[]{:S(2)}) %collective-permute-start.5) | collective-permute-done | bytes 14368 | tf_op jit(solution)/shard_map/ppermute | solution.py:12
  49.1 0.0 collective-permute-start.6
  49.1 0.0 copy-done
  49.1 0.0 copy-done.4
  49.1 0.7 dynamic-slice.2
  49.8 5.9 %collective-permute-done.6 = bf16[1,7168]{1,0:T(2,128)(2,1)S(1)} collective-permute-done((bf16[1,7168]{1,0:T(2,128)(2,1)S(1)}, bf16[1,7168]{1,0:T(2,128)(2,1)S(1)}, u32[]{:S(2)}, u32[]{:S(2)}) %collective-permute-start.6) | collective-permute-done | bytes 14368 | tf_op jit(solution)/shard_map/ppermute | solution.py:12
  55.6 0.7 concatenate.6
  56.4 0.6 gather_fusion
  57.0 0.0 all-gather.4.cloned.1.call-done
  57.0 1.9 %fusion.4 = f32[8,128]{1,0:T(8,128)S(1)} fusion(bf16[7168,128]{1,0:T(8,128)(2,1)} %all-gather.4.cloned.1.call-done, bf16[8,7168]{1,0:T(8,128)(2,1)S(1)} %gather_fusion, pred[8]{0:T(512)(128)(4,1)S(1)} %compare_and_fusion), kind=kOutput, calls=%fused_computation.9 | convolution fusion | flops 14737408 | bytes 1953800 | tf_op jit(solution)/shard_map/dot_general | solution.py:33
  58.9 0.0 all-gather.6.cloned.1.call-done
  58.9 0.0 all-gather.8.cloned.1.call-done
  59.0 2.8 %fusion = f32[8,7168]{1,0:T(8,128)S(1)} fusion(bf16[128,7168]{1,0:T(8,128)(2,1)} %all-gather.8.cloned.1.call-done, bf16[7168,128]{1,0:T(8,128)(2,1)} %all-gather.6.cloned.1.call-done, f32[7168]{0:T(1024)S(1)} %bitcast.13, f32[8]{0:T(128)S(1)} %fusion.11, bf16[8,7168]{1,0:T(8,128)(2,1)S(1)} %gather_fusion, pred[8]{0:T(512)(128)(4,1)S(1)} %compare_and_fusion, ...), kind=kOutput, calls=%fused_computation.3 | convolution fusion | flops 29538304 | bytes 4046888 | tf_op jit(solution)/shard_map/dot_general | solution.py:47
  61.8 0.9 scatter_custom_fusion
  62.7 35.3 %all-reduce.2 = bf16[8,7168]{1,0:T(8,128)(2,1)S(1)} all-reduce(f32[8,7168]{1,0:T(8,128)S(1)} %scatter_custom_fusion), channel_id=2, replica_groups=mesh['groups'=2,'fsdp'=2,'ep'=8] {'ep'}, use_global_device_ids=true, to_apply=%region_1.2.clone | all-reduce | flops 57344 | bytes 344064
  98.0 1.3 %dynamic-slice_convert_fusion = bf16[1,7168]{1,0:T(2,128)(2,1)} fusion(bf16[8,7168]{1,0:T(8,128)(2,1)S(1)} %all-reduce.2, u32[]{:T(128)} %bitcast.5), kind=kLoop, calls=%fused_computation.10 | loop fusion | bytes 28676 | tf_op jit(solution)/shard_map/convert_element_type | solution.py:56
  (6 shorter events, 0.1 us)
Async XLA Ops:
  6.5 42.6 %copy-start = (f32[2,1,8]{2,1,0:T(1,128)S(1)}, f32[2,1,8]{2,1,0:T(1,128)}, u32[]{:S(2)}) copy-start(f32[2,1,8]{2,1,0:T(1,128)} %param.13) | copy-start | bytes 196
  6.5 42.6 %copy-start.4 = (u32[32]{0:T(128)S(1)}, u32[32]{0:T(128)}, u32[]{:S(2)}) copy-start(u32[32]{0:T(128)} %constant.97) | copy-start | bytes 388
  6.5 1.5 %copy-start.1 = (bf16[1,7168]{1,0:T(2,128)(2,1)S(1)}, bf16[1,7168]{1,0:T(2,128)(2,1)}, u32[]{:S(2)}) copy-start(bf16[1,7168]{1,0:T(2,128)(2,1)} %param.7) | copy-start | bytes 43012
  6.5 16.0 %copy-start.2 = (bf16[1,7168]{1,0:T(2,128)(2,1)S(1)}, bf16[1,7168]{1,0:T(2,128)(2,1)}, u32[]{:S(2)}) copy-start(bf16[1,7168]{1,0:T(2,128)(2,1)} %param.11) | copy-start | bytes 43012
  6.5 22.6 %copy-start.3 = (s32[2,1,8]{2,1,0:T(1,128)S(1)}, s32[2,1,8]{2,1,0:T(1,128)}, u32[]{:S(2)}) copy-start(s32[2,1,8]{2,1,0:T(1,128)} %param.12) | copy-start | bytes 196
  6.5 50.5 %all-gather.4.cloned.1.call-start = ((), (), s32[]{:S(2)}) async-start(), calls=%async_computation | async-start | bytes 2752512 | tf_op jit(solution)/shard_map/all_gather | solution.py:35
  7.3 51.7 %all-gather.6.cloned.1.call-start = ((), (), s32[]{:S(2)}) async-start(), calls=%async_computation.1 | async-start | bytes 2752512 | tf_op jit(solution)/shard_map/all_gather | solution.py:40
  8.0 50.9 %all-gather.8.cloned.1.call-start = ((), (), s32[]{:S(2)}) async-start(), calls=%async_computation.2 | async-start | bytes 2752512 | tf_op jit(solution)/shard_map/all_gather | solution.py:49
  8.1 7.9 %collective-permute-start = (bf16[1,7168]{1,0:T(2,128)(2,1)S(1)}, bf16[1,7168]{1,0:T(2,128)(2,1)S(1)}, u32[]{:S(2)}, u32[]{:S(2)}) collective-permute-start(bf16[1,7168]{1,0:T(2,128)(2,1)S(1)} %copy-done.1), channel_id=1, source_target_pairs={{0,1},{1,2},{2,3},{3,4},{4,5},{5,6},{6,7},{7,0},{8,9},{9,10},{10,1... | collective-permute-start | bytes 43016 | tf_op jit(solution)/shard_map/ppermute | solution.py:12
  16.0 6.6 %collective-permute-start.1 = (bf16[1,7168]{1,0:T(2,128)(2,1)S(1)}, bf16[1,7168]{1,0:T(2,128)(2,1)S(1)}, u32[]{:S(2)}, u32[]{:S(2)}) collective-permute-start(bf16[1,7168]{1,0:T(2,128)(2,1)S(1)} %collective-permute-done), channel_id=1, source_target_pairs={{0,1},{1,2},{2,3},{3,4},{4,5},{5,6},{6,7},{7,0},{8,9},{9,10},{10,1... | collective-permute-start | bytes 43016 | tf_op jit(solution)/shard_map/ppermute | solution.py:12
  22.5 6.6 %collective-permute-start.2 = (bf16[1,7168]{1,0:T(2,128)(2,1)S(1)}, bf16[1,7168]{1,0:T(2,128)(2,1)S(1)}, u32[]{:S(2)}, u32[]{:S(2)}) collective-permute-start(bf16[1,7168]{1,0:T(2,128)(2,1)S(1)} %collective-permute-done.1), channel_id=1, source_target_pairs={{0,1},{1,2},{2,3},{3,4},{4,5},{5,6},{6,7},{7,0},{8,9},{9,10},{10,1... | collective-permute-start | bytes 43016 | tf_op jit(solution)/shard_map/ppermute | solution.py:12
  29.1 6.6 %collective-permute-start.3 = (bf16[1,7168]{1,0:T(2,128)(2,1)S(1)}, bf16[1,7168]{1,0:T(2,128)(2,1)S(1)}, u32[]{:S(2)}, u32[]{:S(2)}) collective-permute-start(bf16[1,7168]{1,0:T(2,128)(2,1)S(1)} %collective-permute-done.2), channel_id=1, source_target_pairs={{0,1},{1,2},{2,3},{3,4},{4,5},{5,6},{6,7},{7,0},{8,9},{9,10},{10,1... | collective-permute-start | bytes 43016 | tf_op jit(solution)/shard_map/ppermute | solution.py:12
  35.7 6.8 %collective-permute-start.4 = (bf16[1,7168]{1,0:T(2,128)(2,1)S(1)}, bf16[1,7168]{1,0:T(2,128)(2,1)S(1)}, u32[]{:S(2)}, u32[]{:S(2)}) collective-permute-start(bf16[1,7168]{1,0:T(2,128)(2,1)S(1)} %collective-permute-done.3), channel_id=1, source_target_pairs={{0,1},{1,2},{2,3},{3,4},{4,5},{5,6},{6,7},{7,0},{8,9},{9,10},{10,1... | collective-permute-start | bytes 43016 | tf_op jit(solution)/shard_map/ppermute | solution.py:12
  42.5 6.6 %collective-permute-start.5 = (bf16[1,7168]{1,0:T(2,128)(2,1)S(1)}, bf16[1,7168]{1,0:T(2,128)(2,1)S(1)}, u32[]{:S(2)}, u32[]{:S(2)}) collective-permute-start(bf16[1,7168]{1,0:T(2,128)(2,1)S(1)} %collective-permute-done.4), channel_id=1, source_target_pairs={{0,1},{1,2},{2,3},{3,4},{4,5},{5,6},{6,7},{7,0},{8,9},{9,10},{10,1... | collective-permute-start | bytes 43016 | tf_op jit(solution)/shard_map/ppermute | solution.py:12
  49.1 6.6 %collective-permute-start.6 = (bf16[1,7168]{1,0:T(2,128)(2,1)S(1)}, bf16[1,7168]{1,0:T(2,128)(2,1)S(1)}, u32[]{:S(2)}, u32[]{:S(2)}) collective-permute-start(bf16[1,7168]{1,0:T(2,128)(2,1)S(1)} %collective-permute-done.5), channel_id=1, source_target_pairs={{0,1},{1,2},{2,3},{3,4},{4,5},{5,6},{6,7},{7,0},{8,9},{9,10},{10,1... | collective-permute-start | bytes 43016 | tf_op jit(solution)/shard_map/ppermute | solution.py:12
Sparse Core Ops, SparseCore 0:
  8.9 12.8 all-gather.3
  23.4 11.3 all-gather.5
  36.3 11.3 all-gather.7
